TPU v7x, 32 devices: a whole 2x2x4 slice. The times are simulated.
32 devices in a mesh: rep: 2 (over core), dp: 4 (over y, x), seq: 4 (over z).
Axes of the slice: x: 2, y: 2, z: 4, core: 2. Of those that a mesh axis runs over, the one named last changes fastest.
Arguments:
- tokens: bfloat16 [2, 4, 2048, 2048], P(None, 'dp', ('rep', 'seq')), may hold values from -6 to 6
- lengths: int32 [2, 4], P(None, 'dp'), may hold values from 512 to 2048, as said below
- memory: float32 [2, 4, 16, 128, 128], P(None, 'dp'), may hold values from -48 to 48
- normalizer: float32 [2, 4, 16, 128], P(None, 'dp'), may hold values from 0.5 to 4
- qkv_weight: bfloat16 [6144, 2048], P(('dp', 'seq')), may hold values from -0.1875 to 0.1875
- out_weight: bfloat16 [2048, 2048], P(('dp', 'seq')), may hold values from -0.375 to 0.375
- norm_gains: bfloat16 [2, 2048], P(None, ('dp', 'seq')), may hold values from 0.5 to 1.5
- gate_logit: float32 [16], replicated, may hold values from -2 to 2
- inner_weight: bfloat16 [8192, 4096], P(('dp', 'seq')), may hold values from -0.125 to 0.125
- down_weight: bfloat16 [8192, 2048], P(('dp', 'seq')), may hold values from -0.125 to 0.125
- cotangent: bfloat16 [2, 4, 2048, 2048], P(None, 'dp', ('rep', 'seq')), may hold values from -6 to 6
Outputs:
- output: bfloat16 [2, 4, 2048, 2048], P(None, 'dp', ('rep', 'seq'))
- new_memory: float32 [2, 4, 16, 128, 128], P(None, 'dp', ('rep', 'seq'))
- new_normalizer: float32 [2, 4, 16, 128], P(None, 'dp', ('rep', 'seq'))
- grad_tokens: bfloat16 [2, 4, 2048, 2048], P(None, 'dp', ('rep', 'seq'))
- grad_qkv: float32 [6144, 2048], P(('dp', 'seq'))
- grad_out: float32 [2048, 2048], P(('dp', 'seq'))
- grad_gains: float32 [2, 2048], P(None, ('dp', 'seq'))
- grad_gate: float32 [16], replicated
- grad_inner: float32 [8192, 4096], P(('dp', 'seq'))
- grad_down: float32 [8192, 2048], P(('dp', 'seq'))
Inputs may be any that keep to these rules, and one draw needn't show every extreme that they name: `lengths`: in every draw some sequence has length 2048 and some has 512.
All inputs are finite; a program needn't handle non-finite values.
Results may differ from a plain program's by a relative error of at most 0.018.
The roundings to bfloat16 on the way count: a program that leaves them out, or rounds other values in their place, can miss the bound.
Values may be sent and summed in bfloat16 or wider, within the bound.
A program may use at most 640 MiB of HBM per device.

v0:
```python
import jax
import jax.numpy as jnp
from jax import lax
from jax.sharding import PartitionSpec as P

EPSILON = 1e-05
HIGHEST = lax.Precision.HIGHEST


def contract(left_side, right_side):
    return lax.dot_general(
        left_side, right_side, (((1,), (1,)), ((), ())), preferred_element_type=jnp.float32
    )


def across(left_side, right_side):
    return lax.dot_general(
        left_side, right_side, (((0,), (0,)), ((), ())), preferred_element_type=jnp.float32
    )


def inverse_rms(values):
    return lax.rsqrt(jnp.mean(values * values, axis=-1, keepdims=True) + EPSILON)


def norm_back(grad_normed, normed, scale):
    return scale * (grad_normed - normed * jnp.mean(grad_normed * normed, axis=-1, keepdims=True))


def silu_back(grad_hidden, gates, up_values):
    sigmoid = jax.nn.sigmoid(gates)
    grad_gate = grad_hidden * up_values * sigmoid * (1.0 + gates * (1.0 - sigmoid))
    grad_up = grad_hidden * jax.nn.silu(gates)
    return (grad_gate.astype(jnp.bfloat16), grad_up.astype(jnp.bfloat16))


def spread_terms(attn_terms):
    return (
        lax.psum_scatter(attn_terms[0], ("dp", "seq"), scatter_dimension=0, tiled=True),
        lax.psum_scatter(attn_terms[1], ("dp", "seq"), scatter_dimension=0, tiled=True),
        lax.psum_scatter(attn_terms[2], ("dp", "seq"), scatter_dimension=1, tiled=True),
    )


def shards(
    tokens,
    lengths,
    memory,
    normalizer,
    qkv_weight,
    out_weight,
    norm_gains,
    gate_logit,
    inner_weight,
    down_weight,
    cotangent,
):
    span_rows = tokens.shape[2]
    model_width = tokens.shape[3]
    head_count = gate_logit.shape[0]
    head_dim = model_width // head_count
    seq_parts = lax.axis_size(("rep", "seq"))
    full_length = span_rows * seq_parts
    local_units = inner_weight.shape[0]
    heads_here = head_count // seq_parts
    score_scale = head_dim ** (-0.5)
    qkv_all, out_all, gains_all = (
        lax.all_gather(qkv_weight, ("dp", "seq"), axis=0, tiled=True),
        lax.all_gather(out_weight, ("dp", "seq"), axis=0, tiled=True),
        lax.all_gather(norm_gains, ("dp", "seq"), axis=1, tiled=True),
    )
    gain_one = gains_all[0].astype(jnp.float32)
    gain_two = gains_all[1].astype(jnp.float32)
    span_index = lax.axis_index(("rep", "seq"))
    positions = span_index * span_rows + jnp.arange(span_rows)
    key_positions = jnp.arange(full_length)
    gate_share = jax.nn.sigmoid(gate_logit)
    mixing = gate_share[None, :, None]
    gate_local = inner_weight[:, :model_width]
    up_local = inner_weight[:, model_width:]
    head_start = span_index * heads_here

    def one_micro(micro_carry, inputs):
        total_attn, total_inner, total_gate = micro_carry
        rows_in, length, mem_state, norm_state, grad_rows = inputs
        rows_float = rows_in.astype(jnp.float32)
        scale_one = inverse_rms(rows_float)
        normed_one = rows_float * scale_one
        hidden_one = (normed_one * gain_one).astype(jnp.bfloat16)
        projected = contract(hidden_one, qkv_all).astype(jnp.bfloat16)
        queries = projected[:, :model_width].reshape(span_rows, head_count, head_dim)
        key_rows = projected[:, model_width : 2 * model_width].reshape(
            span_rows, head_count, head_dim
        )
        value_rows = projected[:, 2 * model_width :].reshape(span_rows, head_count, head_dim)
        query_float = queries.astype(jnp.float32)
        query_sig = jax.nn.elu(query_float) + 1.0
        numerator = jnp.einsum("thd,hde->the", query_sig, mem_state, precision=HIGHEST)
        denominator = jnp.einsum("thd,hd->th", query_sig, norm_state, precision=HIGHEST)
        mem_read = numerator / denominator[..., None]
        keys_all, values_all = (
            lax.all_gather(key_rows, ("rep", "seq"), axis=0, tiled=True),
            lax.all_gather(value_rows, ("rep", "seq"), axis=0, tiled=True),
        )
        allowed = (key_positions[None, :] <= positions[:, None]) & (key_positions[None, :] < length)

        def attention_scores():
            raw_scores = (
                jnp.einsum("qhd,khd->hqk", queries, keys_all, preferred_element_type=jnp.float32)
                * score_scale
            )
            return jnp.where(allowed[None], raw_scores, -1e30)

        scores = attention_scores()
        row_max = jnp.max(scores, axis=-1, keepdims=True)
        shifted = jnp.exp(scores - row_max)
        row_total = jnp.sum(shifted, axis=-1, keepdims=True)
        probs_low = (shifted / row_total).astype(jnp.bfloat16)
        dot_read = jnp.einsum(
            "hqk,khd->qhd", probs_low, values_all, preferred_element_type=jnp.float32
        )
        mixed_low = (
            (mixing * mem_read + (1.0 - mixing) * dot_read)
            .reshape(span_rows, model_width)
            .astype(jnp.bfloat16)
        )
        after_attn = rows_float + contract(mixed_low, out_all)
        scale_two = inverse_rms(after_attn)
        normed_two = after_attn * scale_two
        hidden_two = (normed_two * gain_two).astype(jnp.bfloat16)
        rows_all = lax.all_gather(hidden_two, ("dp", "seq"), axis=0, tiled=True)
        gates_kept = contract(rows_all, gate_local)
        ups_kept = contract(rows_all, up_local)
        hidden_kept = (jax.nn.silu(gates_kept) * ups_kept).astype(jnp.bfloat16)
        mlp_out = lax.psum_scatter(
            jnp.dot(hidden_kept, down_weight, preferred_element_type=jnp.float32),
            ("dp", "seq"),
            scatter_dimension=0,
            tiled=True,
        )
        output_rows = (after_attn + mlp_out).astype(jnp.bfloat16)
        key_sig = jax.nn.elu(key_rows.astype(jnp.float32)) + 1.0
        recalled = (
            jnp.einsum("thd,hde->the", key_sig, mem_state, precision=HIGHEST)
            / jnp.einsum("thd,hd->th", key_sig, norm_state, precision=HIGHEST)[..., None]
        )
        live_rows = (positions < length).astype(jnp.float32)
        kept_sig = key_sig * live_rows[:, None, None]
        memory_term = jnp.einsum(
            "thd,the->hde", kept_sig, value_rows.astype(jnp.float32) - recalled, precision=HIGHEST
        )
        norm_term = jnp.sum(kept_sig, axis=0)
        memory_add, norm_add = (
            lax.psum_scatter(
                memory_term.astype(jnp.bfloat16), ("rep", "seq"), scatter_dimension=0, tiled=True
            ).astype(jnp.float32),
            lax.psum_scatter(
                norm_term.astype(jnp.bfloat16), ("rep", "seq"), scatter_dimension=0, tiled=True
            ).astype(jnp.float32),
        )
        new_state = lax.dynamic_slice_in_dim(mem_state, head_start, heads_here, 0) + memory_add
        new_norm = lax.dynamic_slice_in_dim(norm_state, head_start, heads_here, 0) + norm_add
        cot_live = grad_rows.astype(jnp.float32) * live_rows[:, None]
        grad_mlp = cot_live.astype(jnp.bfloat16)
        grad_all = lax.all_gather(grad_mlp, ("dp", "seq"), axis=0, tiled=True)
        grad_hidden = contract(grad_all, down_weight)
        grad_gates, grad_ups = silu_back(grad_hidden, gates_kept, ups_kept)
        inner_term = jnp.concatenate(
            [
                across(grad_gates, rows_all),
                across(grad_ups, rows_all),
                across(hidden_kept, grad_all),
            ],
            axis=1,
        )
        grad_two = lax.psum_scatter(
            jnp.dot(grad_gates, gate_local, preferred_element_type=jnp.float32)
            + jnp.dot(grad_ups, up_local, preferred_element_type=jnp.float32),
            ("dp", "seq"),
            scatter_dimension=0,
            tiled=True,
        )
        grad_after = cot_live + norm_back(grad_two * gain_two, normed_two, scale_two)
        grad_branch = grad_after.astype(jnp.bfloat16)
        grad_mixed = jnp.dot(grad_branch, out_all, preferred_element_type=jnp.float32).astype(
            jnp.bfloat16
        )
        grad_mixed_float = grad_mixed.astype(jnp.float32).reshape(span_rows, head_count, head_dim)
        grad_dot = (grad_mixed_float * (1.0 - mixing)).astype(jnp.bfloat16)
        gate_term = (
            jnp.sum(grad_mixed_float * (mem_read - dot_read), axis=(0, 2))
            * gate_share
            * (1.0 - gate_share)
        )
        probabilities = jnp.exp(attention_scores() - row_max) / row_total
        grad_probs = jnp.einsum(
            "qhd,khd->hqk", grad_dot, values_all, preferred_element_type=jnp.float32
        )
        inner_sum = jnp.sum(probabilities * grad_probs, axis=-1, keepdims=True)
        grad_scores = (probabilities * (grad_probs - inner_sum) * score_scale).astype(jnp.bfloat16)
        grad_query_dot = jnp.einsum(
            "hqk,khd->qhd", grad_scores, keys_all, preferred_element_type=jnp.float32
        )
        grad_keys_all = jnp.einsum(
            "hqk,qhd->khd", grad_scores, queries, preferred_element_type=jnp.float32
        )
        grad_values_all = jnp.einsum(
            "hqk,qhd->khd", probs_low, grad_dot, preferred_element_type=jnp.float32
        )
        grad_keys, grad_values = (
            lax.psum_scatter(
                grad_keys_all.astype(jnp.bfloat16), ("rep", "seq"), scatter_dimension=0, tiled=True
            ).astype(jnp.float32),
            lax.psum_scatter(
                grad_values_all.astype(jnp.bfloat16),
                ("rep", "seq"),
                scatter_dimension=0,
                tiled=True,
            ).astype(jnp.float32),
        )
        grad_read = grad_mixed_float * mixing
        grad_numer = grad_read / denominator[..., None]
        grad_denom = -jnp.sum(grad_read * numerator, axis=-1) / (denominator * denominator)
        grad_sig = (
            jnp.einsum("the,hde->thd", grad_numer, mem_state, precision=HIGHEST)
            + grad_denom[..., None] * norm_state[None]
        )
        elu_slope = jnp.where(query_float > 0.0, 1.0, jnp.exp(jnp.minimum(query_float, 0.0)))
        grad_queries = grad_query_dot + grad_sig * elu_slope
        grad_projected = jnp.concatenate(
            [
                grad_queries.reshape(span_rows, model_width),
                grad_keys.reshape(span_rows, model_width),
                grad_values.reshape(span_rows, model_width),
            ],
            axis=1,
        ).astype(jnp.bfloat16)
        grad_one = jnp.dot(grad_projected, qkv_all, preferred_element_type=jnp.float32)
        grad_tokens_rows = (
            grad_after + norm_back(grad_one * gain_one, normed_one, scale_one)
        ).astype(jnp.bfloat16)
        qkv_term = across(grad_projected, hidden_one)
        out_term = across(grad_branch, mixed_low)
        gains_term = jnp.stack(
            [jnp.sum(grad_one * normed_one, axis=0), jnp.sum(grad_two * normed_two, axis=0)]
        )
        attn_terms = (qkv_term, out_term, gains_term)
        total_attn = tuple((running + share for running, share in zip(total_attn, attn_terms)))
        total_inner = total_inner + inner_term
        total_gate = total_gate + gate_term
        return (
            (total_attn, total_inner, total_gate),
            (output_rows, new_state, new_norm, grad_tokens_rows),
        )

    attn_start = (
        jnp.zeros(qkv_all.shape, jnp.float32),
        jnp.zeros(out_all.shape, jnp.float32),
        jnp.zeros(gains_all.shape, jnp.float32),
    )
    carry_start = (
        attn_start,
        jnp.zeros((local_units, 3 * model_width), jnp.float32),
        jnp.zeros((head_count,), jnp.float32),
    )
    carry_end, stacked = lax.scan(
        one_micro,
        carry_start,
        (tokens[:, 0], lengths[:, 0], memory[:, 0], normalizer[:, 0], cotangent[:, 0]),
    )
    total_attn, total_inner, total_gate = carry_end
    total_attn = spread_terms(total_attn)
    grad_qkv, grad_out, grad_gains, grad_units = (
        lax.psum(total_attn[0].astype(jnp.bfloat16), "rep").astype(jnp.float32),
        lax.psum(total_attn[1].astype(jnp.bfloat16), "rep").astype(jnp.float32),
        lax.psum(total_attn[2].astype(jnp.bfloat16), "rep").astype(jnp.float32),
        lax.psum(total_inner.astype(jnp.bfloat16), "rep").astype(jnp.float32),
    )
    grad_gate = lax.psum(total_gate, ("rep", "dp", "seq"))
    outputs, memories, norm_states, grad_tokens = stacked
    return (
        outputs[:, None],
        memories[:, None],
        norm_states[:, None],
        grad_tokens[:, None],
        grad_qkv,
        grad_out,
        grad_gains,
        grad_gate,
        grad_units[:, : 2 * model_width],
        grad_units[:, 2 * model_width :],
    )


def solution(mesh):
    placed = (
        P(None, "dp", ("rep", "seq"), None),
        P(None, "dp"),
        P(None, "dp", None, None, None),
        P(None, "dp", None, None),
        P(("dp", "seq"), None),
        P(("dp", "seq"), None),
        P(None, ("dp", "seq")),
        P(),
        P(("dp", "seq"), None),
        P(("dp", "seq"), None),
        P(None, "dp", ("rep", "seq"), None),
    )
    return jax.shard_map(
        shards,
        mesh=mesh,
        in_specs=placed,
        out_specs=(
            P(None, "dp", ("rep", "seq"), None),
            P(None, "dp", ("rep", "seq"), None, None),
            P(None, "dp", ("rep", "seq"), None),
            P(None, "dp", ("rep", "seq"), None),
            P(("dp", "seq"), None),
            P(("dp", "seq"), None),
            P(None, ("dp", "seq")),
            P(),
            P(("dp", "seq"), None),
            P(("dp", "seq"), None),
        ),
        check_vma=False,
    )
```

profile of v0, /device:TPU:0, one launch (start us, length us, event | category | flops | bytes accessed | tf_op | source)
XLA Modules:
  0.0 6498.8 jit_solution(5619045800706865099)
XLA Ops:
  10.7 42.4 all_gather.37
  59.2 67.3 %all-gather.9.cloned.1.call-done = bf16[2048,2048]{1,0:T(8,128)(2,1)} async-done(((bf16[128,2048]{1,0:T(8,128)(2,1)}), bf16[2048,2048]{1,0:T(8,128)(2,1)}) %all-gather.9.cloned.1.call-update) | async-done | bytes 8388624 | tf_op jit(solution)/shard_map/all_gather | solution.py:69
  126.4 272.3 %all-gather.7.cloned.1.call-done = bf16[6144,2048]{1,0:T(8,128)(2,1)} async-done(((bf16[384,2048]{1,0:T(8,128)(2,1)}), bf16[6144,2048]{1,0:T(8,128)(2,1)}) %all-gather.7.cloned.1.call-update) | async-done | bytes 25165840 | tf_op jit(solution)/shard_map/all_gather | solution.py:68
  398.8 4900.5 %while.31 = (s32[]{:T(128)}, f32[6144,2048]{1,0:T(8,128)}, f32[2048,2048]{1,0:T(8,128)}, f32[2,2048]{1,0:T(2,128)}, f32[512,6144]{1,0:T(8,128)}, /*index=5*/f32[...) while((s32[]{:T(128)}, f32[6144,2048]{1,0:T(8,128)}, ...), condition=%wide.region_19.20_spmd.clone.clone, body=%wide.region_0.19_spmd.clone.clone.sunk | while | flops 119561093120 | bytes 1664443648 | solution.py:266
  432.1 64.9 all-gather.13.cloned.1.call-done
  515.8 64.4 all-gather.11.cloned.1.call-done
  606.5 166.0 %all-gather.17.cloned.1.call-done = bf16[4096,2048]{1,0:T(8,128)(2,1)} async-done(((bf16[256,2048]{1,0:T(8,128)(2,1)}), bf16[4096,2048]{1,0:T(8,128)(2,1)}) %all-gather.17.cloned.1.call-update) | async-done | bytes 16777232 | tf_op jit(solution)/shard_map/while/body/eval_jaxpr/all_gather | solution.py:165
  787.1 178.5 %all-gather.15.cloned.1.call-done = bf16[4096,2048]{1,0:T(8,128)(2,1)} async-done(((bf16[256,2048]{1,0:T(8,128)(2,1)}), bf16[4096,2048]{1,0:T(8,128)(2,1)}) %all-gather.15.cloned.1.call-update) | async-done | bytes 16777232 | tf_op jit(solution)/shard_map/while/body/eval_jaxpr/all_gather | solution.py:131
  1022.7 26.8 convolution_add_fusion.2
  1080.8 656.8 %reduce-scatter.17.cloned.1.call-done = f32[256,2048]{1,0:T(8,128)} async-done(((f32[4096,2048]{1,0:T(8,128)}), f32[256,2048]{1,0:T(8,128)}) %reduce-scatter.17.cloned.1.call-update) | async-done | bytes 2097168 | tf_op jit(solution)/shard_map/while/body/eval_jaxpr/reduce_scatter | solution.py:176
  1787.6 46.4 convert_bitcast_fusion.6
  1907.3 556.2 %reduce-scatter.23.cloned.1.call-done = f32[256,2048]{1,0:T(8,128)} async-done(((f32[4096,2048]{1,0:T(8,128)}), f32[256,2048]{1,0:T(8,128)}) %reduce-scatter.23.cloned.1.call-update) | async-done | bytes 2097168 | tf_op jit(solution)/shard_map/while/body/eval_jaxpr/reduce_scatter | solution.py:135
  2475.9 48.7 fusion.336
  2524.6 107.4 %reduce-scatter.19.cloned.1.call-done = bf16[256,16,128]{0,2,1:T(8,128)(2,1)} async-done(((bf16[2048,16,128]{0,2,1:T(8,128)(2,1)}), bf16[256,16,128]{0,2,1:T(8,128)(2,1)}) %reduce-scatter.19.cloned.1.call-update) | async-done | bytes 1048592 | tf_op jit(solution)/shard_map/while/body/eval_jaxpr/reduce_scatter | solution.py:214
  2632.0 170.3 %reduce-scatter.21.cloned.1.call-done = bf16[256,16,128]{0,2,1:T(8,128)(2,1)} async-done(((bf16[2048,16,128]{0,2,1:T(8,128)(2,1)}), bf16[256,16,128]{0,2,1:T(8,128)(2,1)}) %reduce-scatter.21.cloned.1.call-update) | async-done | bytes 1048592 | tf_op jit(solution)/shard_map/while/body/eval_jaxpr/reduce_scatter | solution.py:211
  2872.6 68.3 %all-gather.13.cloned.1.call-done = bf16[2048,16,128]{2,0,1:T(8,128)(2,1)} async-done(((bf16[256,16,128]{2,0,1:T(8,128)(2,1)}), bf16[2048,16,128]{2,0,1:T(8,128)(2,1)}) %all-gather.13.cloned.1.call-update) | async-done | bytes 8388624 | tf_op jit(solution)/shard_map/while/body/eval_jaxpr/all_gather | solution.py:102
  2959.7 64.5 all-gather.11.cloned.1.call-done
  3050.8 165.8 %all-gather.17.cloned.1.call-done = bf16[4096,2048]{1,0:T(8,128)(2,1)} async-done(((bf16[256,2048]{1,0:T(8,128)(2,1)}), bf16[4096,2048]{1,0:T(8,128)(2,1)}) %all-gather.17.cloned.1.call-update) | async-done | bytes 16777232 | tf_op jit(solution)/shard_map/while/body/eval_jaxpr/all_gather | solution.py:165
  3231.1 178.5 %all-gather.15.cloned.1.call-done = bf16[4096,2048]{1,0:T(8,128)(2,1)} async-done(((bf16[256,2048]{1,0:T(8,128)(2,1)}), bf16[4096,2048]{1,0:T(8,128)(2,1)}) %all-gather.15.cloned.1.call-update) | async-done | bytes 16777232 | tf_op jit(solution)/shard_map/while/body/eval_jaxpr/all_gather | solution.py:131
  3466.7 26.6 convolution_add_fusion.2
  3524.8 656.6 %reduce-scatter.17.cloned.1.call-done = f32[256,2048]{1,0:T(8,128)} async-done(((f32[4096,2048]{1,0:T(8,128)}), f32[256,2048]{1,0:T(8,128)}) %reduce-scatter.17.cloned.1.call-update) | async-done | bytes 2097168 | tf_op jit(solution)/shard_map/while/body/eval_jaxpr/reduce_scatter | solution.py:176
  4231.4 46.4 convert_bitcast_fusion.6
  4355.6 551.3 %reduce-scatter.23.cloned.1.call-done = f32[256,2048]{1,0:T(8,128)} async-done(((f32[4096,2048]{1,0:T(8,128)}), f32[256,2048]{1,0:T(8,128)}) %reduce-scatter.23.cloned.1.call-update) | async-done | bytes 2097168 | tf_op jit(solution)/shard_map/while/body/eval_jaxpr/reduce_scatter | solution.py:135
  4925.3 48.4 fusion.336
  4973.8 101.8 %reduce-scatter.19.cloned.1.call-done = bf16[256,16,128]{0,2,1:T(8,128)(2,1)} async-done(((bf16[2048,16,128]{0,2,1:T(8,128)(2,1)}), bf16[256,16,128]{0,2,1:T(8,128)(2,1)}) %reduce-scatter.19.cloned.1.call-update) | async-done | bytes 1048592 | tf_op jit(solution)/shard_map/while/body/eval_jaxpr/reduce_scatter | solution.py:214
  5075.6 170.1 %reduce-scatter.21.cloned.1.call-done = bf16[256,16,128]{0,2,1:T(8,128)(2,1)} async-done(((bf16[2048,16,128]{0,2,1:T(8,128)(2,1)}), bf16[256,16,128]{0,2,1:T(8,128)(2,1)}) %reduce-scatter.21.cloned.1.call-update) | async-done | bytes 1048592 | tf_op jit(solution)/shard_map/while/body/eval_jaxpr/reduce_scatter | solution.py:211
  5259.6 32.8 select_add_fusion.4
  5310.6 343.0 %reduce-scatter.13.cloned.1.call-done = f32[128,2048]{1,0:T(8,128)} async-done(((f32[2048,2048]{1,0:T(8,128)}), f32[128,2048]{1,0:T(8,128)}) %reduce-scatter.13.cloned.1.call-update) | async-done | bytes 1048592 | tf_op jit(solution)/shard_map/reduce_scatter | solution.py:40
  5655.7 702.8 %reduce-scatter.11.cloned.1.call-done = f32[384,2048]{1,0:T(8,128)} async-done(((f32[6144,2048]{1,0:T(8,128)}), f32[384,2048]{1,0:T(8,128)}) %reduce-scatter.11.cloned.1.call-update) | async-done | bytes 3145744 | tf_op jit(solution)/shard_map/reduce_scatter | solution.py:39
  6362.4 38.9 psum.38
  6401.3 38.2 reduce-scatter.15.cloned.1.call-done
  6443.4 35.5 all-reduce.6.cloned.1.call-done
  (446 shorter events, 739.9 us)
Async XLA Ops:
  7.2 119.2 %all-gather.9.cloned.1.call-start = ((), (), s32[]{:S(2)}) async-start(), calls=%async_computation.9 | async-start | bytes 8912896 | tf_op jit(solution)/shard_map/all_gather | solution.py:69
  7.9 390.8 %all-gather.7.cloned.1.call-start = ((), (), s32[]{:S(2)}) async-start(), calls=%async_computation.8 | async-start | bytes 26738688 | tf_op jit(solution)/shard_map/all_gather | solution.py:68
  398.8 98.3 %all-gather.13.cloned.1.call-start = ((), (), s32[]{:S(2)}) async-start(), calls=%async_computation.15 | async-start | bytes 9437184 | tf_op jit(solution)/shard_map/while/body/eval_jaxpr/all_gather | solution.py:102
  416.7 163.5 %all-gather.11.cloned.1.call-start = ((), (), s32[]{:S(2)}) async-start(), calls=%async_computation.14 | async-start | bytes 9437184 | tf_op jit(solution)/shard_map/while/body/eval_jaxpr/all_gather | solution.py:103
  418.6 354.0 %all-gather.17.cloned.1.call-start = ((), (), s32[]{:S(2)}) async-start(), calls=%async_computation.17 | async-start | bytes 17825792 | tf_op jit(solution)/shard_map/while/body/eval_jaxpr/all_gather | solution.py:165
  422.4 543.2 %all-gather.15.cloned.1.call-start = ((), (), s32[]{:S(2)}) async-start(), calls=%async_computation.16 | async-start | bytes 17825792 | tf_op jit(solution)/shard_map/while/body/eval_jaxpr/all_gather | solution.py:131
  606.5 1131.1 %reduce-scatter.17.cloned.1.call-start = ((), (), s32[]{:S(2)}) async-start(), calls=%async_computation.18 | async-start | bytes 35651584 | tf_op jit(solution)/shard_map/while/body/eval_jaxpr/reduce_scatter | solution.py:176
  1049.5 787.5 %reduce-scatter.25.cloned.1.call-start = ((), (), s32[]{:S(2)}) async-start(), calls=%async_computation.22 | async-start | bytes 589824 | tf_op jit(solution)/shard_map/while/body/eval_jaxpr/reduce_scatter | solution.py:154
  1062.5 1400.9 %reduce-scatter.23.cloned.1.call-start = ((), (), s32[]{:S(2)}) async-start(), calls=%async_computation.21 | async-start | bytes 35651584 | tf_op jit(solution)/shard_map/while/body/eval_jaxpr/reduce_scatter | solution.py:135
  1080.7 656.8 %copy-start.1 = (f32[256,2048]{1,0:T(8,128)S(1)}, f32[256,2048]{1,0:T(8,128)}, u32[]{:S(2)}) copy-start(f32[256,2048]{1,0:T(8,128)} %copy-done) | copy-start | bytes 6291460 | tf_op jit(solution)/shard_map/while
  1080.7 656.8 %copy-start.27 = (f32[2048]{0:T(1024)S(1)}, f32[2048]{0:T(1024)}, u32[]{:S(2)}) copy-start(f32[2048]{0:T(1024)} %copy-done.26) | copy-start | bytes 24580 | tf_op jit(solution)/shard_map/while
  1080.7 656.8 %copy-start.43 = (f32[256]{0:T(256)S(1)}, f32[256]{0:T(256)}, u32[]{:S(2)}) copy-start(f32[256]{0:T(256)} %copy-done.42) | copy-start | bytes 3076 | tf_op jit(solution)/shard_map/while
  1080.8 1551.2 %reduce-scatter.19.cloned.1.call-start = ((), (), s32[]{:S(2)}) async-start(), calls=%async_computation.19 | async-start | bytes 9437184 | tf_op jit(solution)/shard_map/while/body/eval_jaxpr/reduce_scatter | solution.py:214
  1770.1 1032.2 %reduce-scatter.21.cloned.1.call-start = ((), (), s32[]{:S(2)}) async-start(), calls=%async_computation.20 | async-start | bytes 9437184 | tf_op jit(solution)/shard_map/while/body/eval_jaxpr/reduce_scatter | solution.py:211
  2475.9 326.4 %copy-start.35 = (f32[2048]{0:T(1024)S(1)}, f32[2048]{0:T(1024)}, u32[]{:S(2)}) copy-start(f32[2048]{0:T(1024)} %copy-done.34) | copy-start | bytes 24580 | tf_op jit(solution)/shard_map/while
  2475.9 326.4 %copy-start.47 = (f32[256]{0:T(256)S(1)}, f32[256]{0:T(256)}, u32[]{:S(2)}) copy-start(f32[256]{0:T(256)} %copy-done.46) | copy-start | bytes 3076 | tf_op jit(solution)/shard_map/while
  2839.6 101.3 %all-gather.13.cloned.1.call-start = ((), (), s32[]{:S(2)}) async-start(), calls=%async_computation.15 | async-start | bytes 9437184 | tf_op jit(solution)/shard_map/while/body/eval_jaxpr/all_gather | solution.py:102
  2857.6 166.6 %all-gather.11.cloned.1.call-start = ((), (), s32[]{:S(2)}) async-start(), calls=%async_computation.14 | async-start | bytes 9437184 | tf_op jit(solution)/shard_map/while/body/eval_jaxpr/all_gather | solution.py:103
  2859.5 357.1 %all-gather.17.cloned.1.call-start = ((), (), s32[]{:S(2)}) async-start(), calls=%async_computation.17 | async-start | bytes 17825792 | tf_op jit(solution)/shard_map/while/body/eval_jaxpr/all_gather | solution.py:165
  2863.3 546.3 %all-gather.15.cloned.1.call-start = ((), (), s32[]{:S(2)}) async-start(), calls=%async_computation.16 | async-start | bytes 17825792 | tf_op jit(solution)/shard_map/while/body/eval_jaxpr/all_gather | solution.py:131
  3050.7 1130.6 %reduce-scatter.17.cloned.1.call-start = ((), (), s32[]{:S(2)}) async-start(), calls=%async_computation.18 | async-start | bytes 35651584 | tf_op jit(solution)/shard_map/while/body/eval_jaxpr/reduce_scatter | solution.py:176
  3493.3 787.5 %reduce-scatter.25.cloned.1.call-start = ((), (), s32[]{:S(2)}) async-start(), calls=%async_computation.22 | async-start | bytes 589824 | tf_op jit(solution)/shard_map/while/body/eval_jaxpr/reduce_scatter | solution.py:154
  3506.3 1400.6 %reduce-scatter.23.cloned.1.call-start = ((), (), s32[]{:S(2)}) async-start(), calls=%async_computation.21 | async-start | bytes 35651584 | tf_op jit(solution)/shard_map/while/body/eval_jaxpr/reduce_scatter | solution.py:135
  3524.7 656.7 %copy-start.1 = (f32[256,2048]{1,0:T(8,128)S(1)}, f32[256,2048]{1,0:T(8,128)}, u32[]{:S(2)}) copy-start(f32[256,2048]{1,0:T(8,128)} %copy-done) | copy-start | bytes 6291460 | tf_op jit(solution)/shard_map/while
  3524.7 656.7 %copy-start.27 = (f32[2048]{0:T(1024)S(1)}, f32[2048]{0:T(1024)}, u32[]{:S(2)}) copy-start(f32[2048]{0:T(1024)} %copy-done.26) | copy-start | bytes 24580 | tf_op jit(solution)/shard_map/while
  3524.7 656.7 %copy-start.43 = (f32[256]{0:T(256)S(1)}, f32[256]{0:T(256)}, u32[]{:S(2)}) copy-start(f32[256]{0:T(256)} %copy-done.42) | copy-start | bytes 3076 | tf_op jit(solution)/shard_map/while
  3524.7 1550.8 %reduce-scatter.19.cloned.1.call-start = ((), (), s32[]{:S(2)}) async-start(), calls=%async_computation.19 | async-start | bytes 9437184 | tf_op jit(solution)/shard_map/while/body/eval_jaxpr/reduce_scatter | solution.py:214
  4213.8 1031.9 %reduce-scatter.21.cloned.1.call-start = ((), (), s32[]{:S(2)}) async-start(), calls=%async_computation.20 | async-start | bytes 9437184 | tf_op jit(solution)/shard_map/while/body/eval_jaxpr/reduce_scatter | solution.py:211
  5299.3 354.4 %reduce-scatter.13.cloned.1.call-start = ((), (), s32[]{:S(2)}) async-start(), calls=%async_computation.11 | async-start | bytes 17825792 | tf_op jit(solution)/shard_map/reduce_scatter | solution.py:40
  5300.0 1058.5 %reduce-scatter.11.cloned.1.call-start = ((), (), s32[]{:S(2)}) async-start(), calls=%async_computation.10 | async-start | bytes 53477376 | tf_op jit(solution)/shard_map/reduce_scatter | solution.py:39
  5300.8 1138.7 %reduce-scatter.15.cloned.1.call-start = ((), (), s32[]{:S(2)}) async-start(), calls=%async_computation.12 | async-start | bytes 1114112
  5302.2 1176.8 %all-reduce.6.cloned.1.call-start = ((), (), s32[]{:S(2)}) async-start(), calls=%async_computation.13 | async-start | bytes 16777216 | tf_op jit(solution)/shard_map/psum | solution.py:274
  (114 other events, 3321.6 us)
Sparse Core Ops, SparseCore 0:
  10.8 115.5 all-gather.8
  129.3 269.4 all-gather.6
  416.8 80.2 all-gather.12
  499.1 81.0 all-gather.10
  582.8 189.7 all-gather.16
  775.8 189.7 all-gather.14
  1049.6 687.8 reduce-scatter.16
  1740.4 31.3 reduce-scatter.24
  1774.3 689.1 reduce-scatter.22
  2466.3 165.6 reduce-scatter.18
  2634.4 167.8 reduce-scatter.20
  2857.7 83.1 all-gather.12
  2943.1 81.0 all-gather.10
  3026.8 189.7 all-gather.16
  3219.8 189.7 all-gather.14
  3493.4 687.9 reduce-scatter.16
  4184.0 31.3 reduce-scatter.24
  4217.8 689.0 reduce-scatter.22
  4909.9 165.6 reduce-scatter.18
  5077.8 167.8 reduce-scatter.20
  5302.4 351.1 reduce-scatter.12
  5659.6 698.8 reduce-scatter.10
  6361.5 77.9 reduce-scatter.14
  6443.2 35.6 all-reduce.5
where the time goes:
time: 6500 us
  waiting for transfers between devices  5380 us (83%)
  matrix products  829 us (13%)
  blocking collectives  120 us (2%)
  other arithmetic  86.2 us (1%)
    reduce_scatter x2, waiting for transfers between devices, one_micro(): lax.psum_scatter(jnp.dot(grad_gates, gate_local, preferred_element_type=j...  1310 us
    reduce_scatter x2, waiting for transfers between devices, one_micro(): lax.psum_scatter(jnp.dot(hidden_kept, down_weight, preferred_element_type...  1110 us
    reduce_scatter x1, waiting for transfers between devices, spread_terms(): lax.psum_scatter(attn_terms[0], ('dp', 'seq'), scatter_dimension=0, tiled...  703 us
    all_gather x2, waiting for transfers between devices, one_micro(): rows_all = lax.all_gather(hidden_two, ('dp', 'seq'), axis=0, tiled=True)  357 us
    reduce_scatter x1, waiting for transfers between devices, spread_terms(): lax.psum_scatter(attn_terms[1], ('dp', 'seq'), scatter_dimension=0, tiled...  343 us
    reduce_scatter x2, waiting for transfers between devices, one_micro(): lax.psum_scatter(grad_keys_all.astype(jnp.bfloat16), ('rep', 'seq'), scat...  340 us
    all_gather x2, waiting for transfers between devices, one_micro(): grad_all = lax.all_gather(grad_mlp, ('dp', 'seq'), axis=0, tiled=True)  332 us
    all_gather x1, waiting for transfers between devices, shards(): lax.all_gather(qkv_weight, ('dp', 'seq'), axis=0, tiled=True)  272 us
  transfers between devices with their start and end apart: 24, of which 22 were waited for; matrix products, arithmetic and copies ran while one was open for 10% of the time, Pallas kernels for 0%

commit v1 on v0

--- a/solution.py
+++ b/solution.py
@@ -5,6 +5,28 @@
 
 EPSILON = 1e-05
 HIGHEST = lax.Precision.HIGHEST
+
+
+def laid_out(tiles, dim):
+    lengths = list(tiles.shape[1:])
+    lengths[dim] *= tiles.shape[0]
+    return jnp.moveaxis(tiles, 0, dim).reshape(lengths)
+
+
+def ring_gather(array, axis, dim):
+    size = lax.axis_size(axis)
+    pairs = [(i, (i + 1) % size) for i in range(size)]
+    back = [(b, a) for a, b in pairs]
+    lower, upper = ([], [])
+    for step in range(size - 1):
+        if step % 2 == 0:
+            lower.append(lax.ppermute(lower[-1] if lower else array, axis, pairs))
+        else:
+            upper.append(lax.ppermute(upper[-1] if upper else array, axis, back))
+    pieces = jnp.stack([*lower[::-1], array, *upper])
+    shift = lax.axis_index(axis) - len(lower)
+    pieces = pieces[(jnp.arange(size) - shift) % size]
+    return laid_out(pieces, dim)
 
 
 def contract(left_side, right_side):
@@ -162,7 +184,7 @@
         new_norm = lax.dynamic_slice_in_dim(norm_state, head_start, heads_here, 0) + norm_add
         cot_live = grad_rows.astype(jnp.float32) * live_rows[:, None]
         grad_mlp = cot_live.astype(jnp.bfloat16)
-        grad_all = lax.all_gather(grad_mlp, ("dp", "seq"), axis=0, tiled=True)
+        grad_all = ring_gather(grad_mlp, ("dp", "seq"), 0)
         grad_hidden = contract(grad_all, down_weight)
         grad_gates, grad_ups = silu_back(grad_hidden, gates_kept, ups_kept)
         inner_term = jnp.concatenate(

time: 6500 us -> 6880 us (1.058)
  starting transfers between devices: 1.84 us -> 311 us
  local copies, waits for them, and re-layouts: 56.4 us -> 136 us
    ppermute x0 -> x30, waiting for transfers between devices: none -> 642 us  [the longest x16 365 us: ring_gather(): lower.append(lax.ppermute(lower[-1] if lower else array, axis, pairs))]
    all_gather x2, waiting for transfers between devices: 357 us -> 0.01 us  [one_micro(): rows_all = lax.all_gather(hidden_two, ('dp', 'seq'), axis=0, tiled=True)]
    all_gather x2 -> x0, waiting for transfers between devices: 332 us -> none  [one_micro(): grad_all = lax.all_gather(grad_mlp, ('dp', 'seq'), axis=0, tiled=True)]
    ppermute x0 -> x30, starting transfers between devices: none -> 309 us  [the longest x16 292 us: ring_gather(): lower.append(lax.ppermute(lower[-1] if lower else array, axis, pairs))]
  transfers between devices with their start and end apart: 24 -> 52, of which waited for: 22 -> 46; matrix products, arithmetic and copies ran while one was open for 10% -> 10% of each run, Pallas kernels for 0% -> 0%
where the time goes in v1:
time: 6880 us; the launch traced here: 6870 us
  waiting for transfers between devices  5370 us (78%)
  matrix products  828 us (12%)
  starting transfers between devices  311 us (5%)
  local copies, waits for them, and re-layouts  136 us (2%)
  blocking collectives  119 us (2%)
  other arithmetic  84.4 us (1%)
    reduce_scatter x2, waiting for transfers between devices, one_micro(): lax.psum_scatter(jnp.dot(grad_gates, gate_local, preferred_element_type=j...  1350 us
    reduce_scatter x2, waiting for transfers between devices, one_micro(): lax.psum_scatter(jnp.dot(hidden_kept, down_weight, preferred_element_type...  1110 us
    reduce_scatter x1, waiting for transfers between devices, spread_terms(): lax.psum_scatter(attn_terms[0], ('dp', 'seq'), scatter_dimension=0, tiled...  702 us
    ppermute x16, waiting for transfers between devices, ring_gather(): lower.append(lax.ppermute(lower[-1] if lower else array, axis, pairs))  365 us
    reduce_scatter x1, waiting for transfers between devices, spread_terms(): lax.psum_scatter(attn_terms[1], ('dp', 'seq'), scatter_dimension=0, tiled...  343 us
    reduce_scatter x2, waiting for transfers between devices, one_micro(): lax.psum_scatter(grad_keys_all.astype(jnp.bfloat16), ('rep', 'seq'), scat...  340 us
    ppermute x16, starting transfers between devices, ring_gather(): lower.append(lax.ppermute(lower[-1] if lower else array, axis, pairs))  292 us
    ppermute x14, waiting for transfers between devices, ring_gather(): upper.append(lax.ppermute(upper[-1] if upper else array, axis, back))  278 us
  transfers between devices with their start and end apart: 52, of which 46 were waited for; matrix products, arithmetic and copies ran while one was open for 10% of the time, Pallas kernels for 0%

profile of v1, /device:TPU:0, one launch (start us, length us, event | category | flops | bytes accessed | tf_op | source)
XLA Modules:
  0.0 6872.4 jit_solution(8415944367603537793)
XLA Ops:
  11.7 42.4 all_gather.30
  60.1 66.3 all-gather.8.cloned.1.call-done
  126.4 272.3 %all-gather.6.cloned.1.call-done = bf16[6144,2048]{1,0:T(8,128)(2,1)} async-done(((bf16[384,2048]{1,0:T(8,128)(2,1)}), bf16[6144,2048]{1,0:T(8,128)(2,1)}) %all-gather.6.cloned.1.call-update) | async-done | bytes 25165840 | tf_op jit(solution)/shard_map/all_gather | solution.py:90
  398.8 5275.1 %while.31 = (s32[]{:T(128)}, f32[6144,2048]{1,0:T(8,128)}, f32[2048,2048]{1,0:T(8,128)}, f32[2,2048]{1,0:T(2,128)}, f32[512,6144]{1,0:T(8,128)}, /*index=5*/f32[...) while((s32[]{:T(128)}, f32[6144,2048]{1,0:T(8,128)}, ...), condition=%wide.region_19.20_spmd.clone.clone, body=%wide.region_0.19_spmd.clone.clone.sunk | while | flops 119562665984 | bytes 1856330624 | solution.py:288
  431.2 65.9 all-gather.12.cloned.1.call-done
  515.9 64.3 all-gather.10.cloned.1.call-done
  606.6 45.2 collective-permute-done
  690.0 65.2 collective-permute-done.8
  845.9 38.9 collective-permute-start.4
  1251.4 673.5 %reduce-scatter.17.cloned.1.call-done = f32[256,2048]{1,0:T(8,128)} async-done(((f32[4096,2048]{1,0:T(8,128)}), f32[256,2048]{1,0:T(8,128)}) %reduce-scatter.17.cloned.1.call-update) | async-done | bytes 2097168 | tf_op jit(solution)/shard_map/while/body/eval_jaxpr/reduce_scatter | solution.py:198
  1974.9 46.4 convert_bitcast_fusion.7
  2093.2 557.3 %reduce-scatter.23.cloned.1.call-done = f32[256,2048]{1,0:T(8,128)} async-done(((f32[4096,2048]{1,0:T(8,128)}), f32[256,2048]{1,0:T(8,128)}) %reduce-scatter.23.cloned.1.call-update) | async-done | bytes 2097168 | tf_op jit(solution)/shard_map/while/body/eval_jaxpr/reduce_scatter | solution.py:157
  2662.7 48.6 fusion.345
  2711.3 107.8 %reduce-scatter.19.cloned.1.call-done = bf16[256,16,128]{0,2,1:T(8,128)(2,1)} async-done(((bf16[2048,16,128]{0,2,1:T(8,128)(2,1)}), bf16[256,16,128]{0,2,1:T(8,128)(2,1)}) %reduce-scatter.19.cloned.1.call-update) | async-done | bytes 1048592 | tf_op jit(solution)/shard_map/while/body/eval_jaxpr/reduce_scatter | solution.py:236
  2819.2 170.1 %reduce-scatter.21.cloned.1.call-done = bf16[256,16,128]{0,2,1:T(8,128)(2,1)} async-done(((bf16[2048,16,128]{0,2,1:T(8,128)(2,1)}), bf16[256,16,128]{0,2,1:T(8,128)(2,1)}) %reduce-scatter.21.cloned.1.call-update) | async-done | bytes 1048592 | tf_op jit(solution)/shard_map/while/body/eval_jaxpr/reduce_scatter | solution.py:233
  3059.5 68.8 %all-gather.12.cloned.1.call-done = bf16[2048,16,128]{2,0,1:T(8,128)(2,1)} async-done(((bf16[256,16,128]{2,0,1:T(8,128)(2,1)}), bf16[2048,16,128]{2,0,1:T(8,128)(2,1)}) %all-gather.12.cloned.1.call-update) | async-done | bytes 8388624 | tf_op jit(solution)/shard_map/while/body/eval_jaxpr/all_gather | solution.py:124
  3147.1 64.3 all-gather.10.cloned.1.call-done
  3237.8 45.2 collective-permute-done
  3321.1 65.3 collective-permute-done.8
  3477.2 38.8 collective-permute-start.4
  3882.8 673.3 %reduce-scatter.17.cloned.1.call-done = f32[256,2048]{1,0:T(8,128)} async-done(((f32[4096,2048]{1,0:T(8,128)}), f32[256,2048]{1,0:T(8,128)}) %reduce-scatter.17.cloned.1.call-update) | async-done | bytes 2097168 | tf_op jit(solution)/shard_map/while/body/eval_jaxpr/reduce_scatter | solution.py:198
  4606.1 46.4 convert_bitcast_fusion.7
  4728.6 553.0 %reduce-scatter.23.cloned.1.call-done = f32[256,2048]{1,0:T(8,128)} async-done(((f32[4096,2048]{1,0:T(8,128)}), f32[256,2048]{1,0:T(8,128)}) %reduce-scatter.23.cloned.1.call-update) | async-done | bytes 2097168 | tf_op jit(solution)/shard_map/while/body/eval_jaxpr/reduce_scatter | solution.py:157
  5299.9 48.6 fusion.345
  5348.5 101.7 %reduce-scatter.19.cloned.1.call-done = bf16[256,16,128]{0,2,1:T(8,128)(2,1)} async-done(((bf16[2048,16,128]{0,2,1:T(8,128)(2,1)}), bf16[256,16,128]{0,2,1:T(8,128)(2,1)}) %reduce-scatter.19.cloned.1.call-update) | async-done | bytes 1048592 | tf_op jit(solution)/shard_map/while/body/eval_jaxpr/reduce_scatter | solution.py:236
  5450.1 170.1 %reduce-scatter.21.cloned.1.call-done = bf16[256,16,128]{0,2,1:T(8,128)(2,1)} async-done(((bf16[2048,16,128]{0,2,1:T(8,128)(2,1)}), bf16[256,16,128]{0,2,1:T(8,128)(2,1)}) %reduce-scatter.21.cloned.1.call-update) | async-done | bytes 1048592 | tf_op jit(solution)/shard_map/while/body/eval_jaxpr/reduce_scatter | solution.py:233
  5634.2 32.9 select_add_fusion.4
  5685.2 343.0 %reduce-scatter.13.cloned.1.call-done = f32[128,2048]{1,0:T(8,128)} async-done(((f32[2048,2048]{1,0:T(8,128)}), f32[128,2048]{1,0:T(8,128)}) %reduce-scatter.13.cloned.1.call-update) | async-done | bytes 1048592 | tf_op jit(solution)/shard_map/reduce_scatter | solution.py:62
  6030.3 702.4 %reduce-scatter.11.cloned.1.call-done = f32[384,2048]{1,0:T(8,128)} async-done(((f32[6144,2048]{1,0:T(8,128)}), f32[384,2048]{1,0:T(8,128)}) %reduce-scatter.11.cloned.1.call-update) | async-done | bytes 3145744 | tf_op jit(solution)/shard_map/reduce_scatter | solution.py:61
  6736.6 39.1 psum.38
  6775.7 37.8 reduce-scatter.15.cloned.1.call-done
  6817.4 35.9 all-reduce.6.cloned.1.call-done
  (596 shorter events, 1520.2 us)
Async XLA Ops:
  7.2 119.2 %all-gather.8.cloned.1.call-start = ((), (), s32[]{:S(2)}) async-start(), calls=%async_computation.9 | async-start | bytes 8912896 | tf_op jit(solution)/shard_map/all_gather | solution.py:91
  7.9 390.8 %all-gather.6.cloned.1.call-start = ((), (), s32[]{:S(2)}) async-start(), calls=%async_computation.8 | async-start | bytes 26738688 | tf_op jit(solution)/shard_map/all_gather | solution.py:90
  398.8 98.3 %all-gather.12.cloned.1.call-start = ((), (), s32[]{:S(2)}) async-start(), calls=%async_computation.15 | async-start | bytes 9437184 | tf_op jit(solution)/shard_map/while/body/eval_jaxpr/all_gather | solution.py:124
  416.7 163.5 %all-gather.10.cloned.1.call-start = ((), (), s32[]{:S(2)}) async-start(), calls=%async_computation.14 | async-start | bytes 9437184 | tf_op jit(solution)/shard_map/while/body/eval_jaxpr/all_gather | solution.py:125
  419.8 702.9 %all-gather.14.cloned.1.call-start = ((), (), s32[]{:S(2)}) async-start(), calls=%async_computation.16 | async-start | bytes 17825792 | tf_op jit(solution)/shard_map/while/body/eval_jaxpr/all_gather | solution.py:153
  605.7 1319.2 %reduce-scatter.17.cloned.1.call-start = ((), (), s32[]{:S(2)}) async-start(), calls=%async_computation.17 | async-start | bytes 35651584 | tf_op jit(solution)/shard_map/while/body/eval_jaxpr/reduce_scatter | solution.py:198
  652.7 102.6 %collective-permute-start.8 = (bf16[256,2048]{1,0:T(8,128)(2,1)S(1)}, bf16[256,2048]{1,0:T(8,128)(2,1)S(1)}, u32[]{:S(2)}, u32[]{:S(2)}) collective-permute-start(bf16[256,2048]{1,0:T(8,128)(2,1)S(1)} %fusion.335), channel_id=1, source_target_pairs={{1,0},{2,1},{3,2},{4,3},{5,4},{6,5},{7,6},{8,7},{9,8},{10,9},{11,1... | collective-permute-start | bytes 3145736 | tf_op jit(solution)/shard_map/while/body/eval_jaxpr/ppermute | solution.py:25
  681.5 82.6 %collective-permute-start.2 = (bf16[256,2048]{1,0:T(8,128)(2,1)S(1)}, bf16[256,2048]{1,0:T(8,128)(2,1)S(1)}, u32[]{:S(2)}, u32[]{:S(2)}) collective-permute-start(bf16[256,2048]{1,0:T(8,128)(2,1)S(1)} %collective-permute-done.1), channel_id=1, source_target_pairs={{0,1},{1,2},{2,3},{3,4},{4,5},{5,6},{6,7},{7,8},{8,9},{9,10},{10,1... | collective-permute-start | bytes 3145736 | tf_op jit(solution)/shard_map/while/body/eval_jaxpr/ppermute | solution.py:23
  764.1 81.8 %collective-permute-start.3 = (bf16[256,2048]{1,0:T(8,128)(2,1)S(1)}, bf16[256,2048]{1,0:T(8,128)(2,1)S(1)}, u32[]{:S(2)}, u32[]{:S(2)}) collective-permute-start(bf16[256,2048]{1,0:T(8,128)(2,1)S(1)} %collective-permute-done.2), channel_id=1, source_target_pairs={{0,1},{1,2},{2,3},{3,4},{4,5},{5,6},{6,7},{7,8},{8,9},{9,10},{10,1... | collective-permute-start | bytes 3145736 | tf_op jit(solution)/shard_map/while/body/eval_jaxpr/ppermute | solution.py:23
  819.4 96.9 %collective-permute-start.10 = (bf16[256,2048]{1,0:T(8,128)(2,1)S(1)}, bf16[256,2048]{1,0:T(8,128)(2,1)S(1)}, u32[]{:S(2)}, u32[]{:S(2)}) collective-permute-start(bf16[256,2048]{1,0:T(8,128)(2,1)S(1)} %collective-permute-done.9), channel_id=1, source_target_pairs={{1,0},{2,1},{3,2},{4,3},{5,4},{6,5},{7,6},{8,7},{9,8},{10,9},{11,1... | collective-permute-start | bytes 3145736 | tf_op jit(solution)/shard_map/while/body/eval_jaxpr/ppermute | solution.py:25
  845.9 89.9 %collective-permute-start.4 = (bf16[256,2048]{1,0:T(8,128)(2,1)S(1)}, bf16[256,2048]{1,0:T(8,128)(2,1)S(1)}, u32[]{:S(2)}, u32[]{:S(2)}) collective-permute-start(bf16[256,2048]{1,0:T(8,128)(2,1)S(1)} %collective-permute-done.3), channel_id=1, source_target_pairs={{0,1},{1,2},{2,3},{3,4},{4,5},{5,6},{6,7},{7,8},{8,9},{9,10},{10,1... | collective-permute-start | bytes 3145736 | tf_op jit(solution)/shard_map/while/body/eval_jaxpr/ppermute | solution.py:23
  1218.1 806.2 %reduce-scatter.25.cloned.1.call-start = ((), (), s32[]{:S(2)}) async-start(), calls=%async_computation.21 | async-start | bytes 589824 | tf_op jit(solution)/shard_map/while/body/eval_jaxpr/reduce_scatter | solution.py:176
  1232.3 1418.1 %reduce-scatter.23.cloned.1.call-start = ((), (), s32[]{:S(2)}) async-start(), calls=%async_computation.20 | async-start | bytes 35651584 | tf_op jit(solution)/shard_map/while/body/eval_jaxpr/reduce_scatter | solution.py:157
  1251.4 1567.8 %reduce-scatter.19.cloned.1.call-start = ((), (), s32[]{:S(2)}) async-start(), calls=%async_computation.18 | async-start | bytes 9437184 | tf_op jit(solution)/shard_map/while/body/eval_jaxpr/reduce_scatter | solution.py:236
  1957.4 1031.9 %reduce-scatter.21.cloned.1.call-start = ((), (), s32[]{:S(2)}) async-start(), calls=%async_computation.19 | async-start | bytes 9437184 | tf_op jit(solution)/shard_map/while/body/eval_jaxpr/reduce_scatter | solution.py:233
  3027.0 101.3 %all-gather.12.cloned.1.call-start = ((), (), s32[]{:S(2)}) async-start(), calls=%async_computation.15 | async-start | bytes 9437184 | tf_op jit(solution)/shard_map/while/body/eval_jaxpr/all_gather | solution.py:124
  3045.0 166.4 %all-gather.10.cloned.1.call-start = ((), (), s32[]{:S(2)}) async-start(), calls=%async_computation.14 | async-start | bytes 9437184 | tf_op jit(solution)/shard_map/while/body/eval_jaxpr/all_gather | solution.py:125
  3048.1 706.0 %all-gather.14.cloned.1.call-start = ((), (), s32[]{:S(2)}) async-start(), calls=%async_computation.16 | async-start | bytes 17825792 | tf_op jit(solution)/shard_map/while/body/eval_jaxpr/all_gather | solution.py:153
  3236.9 1319.2 %reduce-scatter.17.cloned.1.call-start = ((), (), s32[]{:S(2)}) async-start(), calls=%async_computation.17 | async-start | bytes 35651584 | tf_op jit(solution)/shard_map/while/body/eval_jaxpr/reduce_scatter | solution.py:198
  3283.9 102.6 %collective-permute-start.8 = (bf16[256,2048]{1,0:T(8,128)(2,1)S(1)}, bf16[256,2048]{1,0:T(8,128)(2,1)S(1)}, u32[]{:S(2)}, u32[]{:S(2)}) collective-permute-start(bf16[256,2048]{1,0:T(8,128)(2,1)S(1)} %fusion.335), channel_id=1, source_target_pairs={{1,0},{2,1},{3,2},{4,3},{5,4},{6,5},{7,6},{8,7},{9,8},{10,9},{11,1... | collective-permute-start | bytes 3145736 | tf_op jit(solution)/shard_map/while/body/eval_jaxpr/ppermute | solution.py:25
  3312.7 82.6 %collective-permute-start.2 = (bf16[256,2048]{1,0:T(8,128)(2,1)S(1)}, bf16[256,2048]{1,0:T(8,128)(2,1)S(1)}, u32[]{:S(2)}, u32[]{:S(2)}) collective-permute-start(bf16[256,2048]{1,0:T(8,128)(2,1)S(1)} %collective-permute-done.1), channel_id=1, source_target_pairs={{0,1},{1,2},{2,3},{3,4},{4,5},{5,6},{6,7},{7,8},{8,9},{9,10},{10,1... | collective-permute-start | bytes 3145736 | tf_op jit(solution)/shard_map/while/body/eval_jaxpr/ppermute | solution.py:23
  3395.4 81.8 %collective-permute-start.3 = (bf16[256,2048]{1,0:T(8,128)(2,1)S(1)}, bf16[256,2048]{1,0:T(8,128)(2,1)S(1)}, u32[]{:S(2)}, u32[]{:S(2)}) collective-permute-start(bf16[256,2048]{1,0:T(8,128)(2,1)S(1)} %collective-permute-done.2), channel_id=1, source_target_pairs={{0,1},{1,2},{2,3},{3,4},{4,5},{5,6},{6,7},{7,8},{8,9},{9,10},{10,1... | collective-permute-start | bytes 3145736 | tf_op jit(solution)/shard_map/while/body/eval_jaxpr/ppermute | solution.py:23
  3450.6 96.9 %collective-permute-start.10 = (bf16[256,2048]{1,0:T(8,128)(2,1)S(1)}, bf16[256,2048]{1,0:T(8,128)(2,1)S(1)}, u32[]{:S(2)}, u32[]{:S(2)}) collective-permute-start(bf16[256,2048]{1,0:T(8,128)(2,1)S(1)} %collective-permute-done.9), channel_id=1, source_target_pairs={{1,0},{2,1},{3,2},{4,3},{5,4},{6,5},{7,6},{8,7},{9,8},{10,9},{11,1... | collective-permute-start | bytes 3145736 | tf_op jit(solution)/shard_map/while/body/eval_jaxpr/ppermute | solution.py:25
  3477.2 89.9 %collective-permute-start.4 = (bf16[256,2048]{1,0:T(8,128)(2,1)S(1)}, bf16[256,2048]{1,0:T(8,128)(2,1)S(1)}, u32[]{:S(2)}, u32[]{:S(2)}) collective-permute-start(bf16[256,2048]{1,0:T(8,128)(2,1)S(1)} %collective-permute-done.3), channel_id=1, source_target_pairs={{0,1},{1,2},{2,3},{3,4},{4,5},{5,6},{6,7},{7,8},{8,9},{9,10},{10,1... | collective-permute-start | bytes 3145736 | tf_op jit(solution)/shard_map/while/body/eval_jaxpr/ppermute | solution.py:23
  3849.6 806.0 %reduce-scatter.25.cloned.1.call-start = ((), (), s32[]{:S(2)}) async-start(), calls=%async_computation.21 | async-start | bytes 589824 | tf_op jit(solution)/shard_map/while/body/eval_jaxpr/reduce_scatter | solution.py:176
  3863.8 1417.8 %reduce-scatter.23.cloned.1.call-start = ((), (), s32[]{:S(2)}) async-start(), calls=%async_computation.20 | async-start | bytes 35651584 | tf_op jit(solution)/shard_map/while/body/eval_jaxpr/reduce_scatter | solution.py:157
  3882.8 1567.4 %reduce-scatter.19.cloned.1.call-start = ((), (), s32[]{:S(2)}) async-start(), calls=%async_computation.18 | async-start | bytes 9437184 | tf_op jit(solution)/shard_map/while/body/eval_jaxpr/reduce_scatter | solution.py:236
  4588.6 1031.7 %reduce-scatter.21.cloned.1.call-start = ((), (), s32[]{:S(2)}) async-start(), calls=%async_computation.19 | async-start | bytes 9437184 | tf_op jit(solution)/shard_map/while/body/eval_jaxpr/reduce_scatter | solution.py:233
  5673.9 354.4 %reduce-scatter.13.cloned.1.call-start = ((), (), s32[]{:S(2)}) async-start(), calls=%async_computation.11 | async-start | bytes 17825792 | tf_op jit(solution)/shard_map/reduce_scatter | solution.py:62
  5674.7 1058.1 %reduce-scatter.11.cloned.1.call-start = ((), (), s32[]{:S(2)}) async-start(), calls=%async_computation.10 | async-start | bytes 53477376 | tf_op jit(solution)/shard_map/reduce_scatter | solution.py:61
  5675.2 1138.2 %reduce-scatter.15.cloned.1.call-start = ((), (), s32[]{:S(2)}) async-start(), calls=%async_computation.12 | async-start | bytes 1114112
  5676.8 1176.6 %all-reduce.6.cloned.1.call-start = ((), (), s32[]{:S(2)}) async-start(), calls=%async_computation.13 | async-start | bytes 16777216 | tf_op jit(solution)/shard_map/psum | solution.py:296
  (171 other events, 13507.6 us)
Sparse Core Ops, SparseCore 0:
  10.8 115.5 all-gather.7
  129.3 269.4 all-gather.5
  416.8 80.2 all-gather.11
  499.1 81.0 all-gather.9
  605.8 355.9 all-gather.13
  1218.3 706.6 reduce-scatter.16
  1927.7 31.4 reduce-scatter.24
  1961.7 688.7 reduce-scatter.22
  2653.5 165.6 reduce-scatter.18
  2821.4 167.8 reduce-scatter.20
  3045.1 83.1 all-gather.11
  3130.3 81.0 all-gather.9
  3237.0 355.8 all-gather.13
  3849.7 706.3 reduce-scatter.16
  4558.8 31.3 reduce-scatter.24
  4592.5 689.0 reduce-scatter.22
  5284.4 165.6 reduce-scatter.18
  5452.4 167.8 reduce-scatter.20
  5677.0 351.1 reduce-scatter.12
  6034.1 698.6 reduce-scatter.10
  6735.7 77.7 reduce-scatter.14
  6817.4 35.9 all-reduce.5
